TPU v7x, 512 devices: a whole 4x4x16 slice. The times are simulated.
512 devices in a mesh: row: 32 (over z, core), col: 16 (over y, x).
Axes of the slice: x: 4, y: 4, z: 16, core: 2. Of those that a mesh axis runs over, the one named last changes fastest.
Arguments:
- trailing: bfloat16 [24576, 12288], P('row', 'col'), may hold values from -6 to 6
- offdiagonal_panel_rows: bfloat16 [2, 24576, 512], P(None, ('row', 'col')), may hold values from -3 to 3
- pivot_diagonal_blocks: bfloat16 [2, 512, 512], replicated, may hold values from -3 to 14, as said below
- coupling: bfloat16 [512, 512], replicated, may hold values from -0.3314563 to 0.3314563, as said below
- pattern: int32 [2, 192], replicated, may hold values 0 or 1
- block_slot_lookup: int32 [192], replicated, may hold values from 0 to 191, each once
- elimination_sequence: int32 [2], replicated, may hold values from 0 to 1, each once
Outputs:
- updated: bfloat16 [24576, 12288], P('row', 'col')
- factor: bfloat16 [2, 24576, 512], P(None, ('row', 'col'))
Inputs may be any that keep to these rules, and one draw needn't show every extreme that they name: `pivot_diagonal_blocks`: each diagonal block is symmetric positive definite. `coupling`: pivot_diagonal_blocks[b] - link link^T is positive definite. `elimination_sequence`: a permutation of the two panel indices.
All inputs are finite; a program needn't handle non-finite values.
Results may differ from a plain program's by a relative error of at most 0.0055.
Values may be sent and summed in bfloat16 or wider, within the bound.
No kernel may reach another device: no remote copies, remote signals or barrier semaphores. Data moves between devices by JAX's collectives and lax.ppermute only.
A program may use at most 64 MiB of HBM per device.

v0:
```python
import jax
import jax.numpy as jnp
from jax import lax
from jax.experimental import pallas as pl
from jax.experimental.pallas import tpu as pltpu
from jax.sharding import Mesh, PartitionSpec as P


B = 128
STEP = 16
CHUNK = 384
F32 = jnp.float32
BF16 = jnp.bfloat16


VMEM = pl.BlockSpec(memory_space=pltpu.VMEM)
SMEM = pl.BlockSpec(memory_space=pltpu.SMEM)
ANY = pl.BlockSpec(memory_space=pl.ANY)


def dot(left, right, contract_left, contract_right):
    return lax.dot_general(
        left, right, (((contract_left,), (contract_right,)), ((), ())), preferred_element_type=F32
    )


def split(value):
    high = value.astype(BF16)
    return high, (value - high.astype(F32)).astype(BF16)


def dot_split(left, right, contract_left, contract_right):
    left_high, left_low = split(left)
    right_high, right_low = split(right)
    return (
        dot(left_high, right_high, contract_left, contract_right)
        + dot(left_high, right_low, contract_left, contract_right)
        + dot(left_low, right_high, contract_left, contract_right)
    )


def row_of(value, sublane):
    return jnp.broadcast_to(value[sublane : sublane + 1, :], value.shape)


def eliminate(work, inverse, step):
    start = STEP * step
    tiles = STEP // 8
    rows = [[ref[start + 8 * h : start + 8 * h + 8, :] for h in range(tiles)] for ref in (work, inverse)]
    columns = [
        [
            jnp.broadcast_to(rows[0][h][:, start + j : start + j + 1], (8, B)) if h >= j // 8 else None
            for h in range(tiles)
        ]
        for j in range(STEP)
    ]
    nothing = jnp.minimum(jnp.abs(rows[0][0]), 0.0)
    columns[0] = [column + nothing for column in columns[0]]
    sublane = lax.broadcasted_iota(jnp.int32, (8, B), 0)
    zero = jnp.zeros((8, B), F32)
    scale = [zero] * tiles
    for k in range(STEP):
        tile, s = k // 8, k % 8
        pivot = list(columns[k])
        root = lax.rsqrt(row_of(pivot[tile], s))
        inverse_pivot = root * root
        scale[tile] = jnp.where(sublane == s, root, scale[tile])
        below = [(h, pivot[h]) for h in range(tile + 1, tiles)]
        if s < 7:
            below.append((tile, jnp.where(sublane > s, pivot[tile], zero)))
        for j in range(k + 1, STEP):
            entry = row_of(pivot[j // 8], j % 8)
            if j > k + 1:
                entry = entry * inverse_pivot
            for h, column in below:
                if h >= j // 8:
                    change = column * entry
                    columns[j][h] = columns[j][h] - (change if j > k + 1 else change * inverse_pivot)
        for side in rows:
            pivot_row = row_of(side[tile], s) * inverse_pivot
            for h, column in below:
                side[h] = side[h] - column * pivot_row
    rows = [jnp.concatenate([side[h] * scale[h] for h in range(tiles)], 0) for side in rows]
    work[start : start + STEP, :] = rows[0]
    inverse[start : start + STEP, :] = rows[1]
    if start + STEP == B:
        return
    upper_high, upper_low = split(rows[0])
    side_high, side_low = split(rows[1])
    left = jnp.concatenate([upper_high, upper_high, upper_low], 0)
    rest = slice(start + STEP, B)
    change = dot(left, jnp.concatenate([upper_high, upper_low, upper_high], 0), 0, 0)
    work[rest, :] = work[rest, :] - change[rest, :]
    change = dot(left, jnp.concatenate([side_high, side_low, side_high], 0), 0, 0)
    inverse[rest, :] = inverse[rest, :] - change[rest, :]


def factor(matrix, inverse, block_work, block_inverse):
    size = matrix.shape[0]
    inverse[...] = jnp.zeros(inverse.shape, F32)
    row = lax.broadcasted_iota(jnp.int32, (B, B), 0)
    column = lax.broadcasted_iota(jnp.int32, (B, B), 1)
    for start in range(0, size, B):
        here, rest = slice(start, start + B), slice(start + B, size)
        done = slice(0, start + B)
        block_work[...] = matrix[here, here]
        block_inverse[...] = jnp.where(row == column, 1.0, 0.0).astype(F32)
        for step in range(B // STEP):
            eliminate(block_work, block_inverse, step)
        own = block_inverse[...]
        if start:
            inverse[here, 0:start] = dot_split(own, inverse[here, 0:start], 1, 0)
        inverse[here, here] = own
        if start + B < size:
            upper = dot_split(own, matrix[here, rest], 1, 0)
            matrix[rest, rest] = matrix[rest, rest] - dot_split(upper, upper, 0, 0)
            inverse[rest, done] = inverse[rest, done] - dot_split(upper, inverse[here, done], 0, 0)


def first_kernel(order, blocks, coupling, inverse_out, link_out, matrix, inverse, work, work_inverse, turned):
    first = order[0]
    matrix[...] = blocks[first].astype(F32)
    factor(matrix, inverse, work, work_inverse)
    high, low = split(inverse[...])
    inverse_out[0], inverse_out[1] = high, low

    @pl.when(first == 0)
    def _():
        turned[...] = coupling[...]

    @pl.when(first != 0)
    def _():
        turned[...] = coupling[...].astype(F32).T.astype(BF16)

    kmat = turned[...]
    link_out[...] = (dot(kmat, high, 1, 1) + dot(kmat, low, 1, 1)).astype(BF16)


def second_kernel(order, blocks, link_ref, inverse_out, matrix, inverse, work, work_inverse):
    second = order[1]
    link = link_ref[...]
    matrix[...] = blocks[second].astype(F32) - dot(link, link, 1, 1)
    factor(matrix, inverse, work, work_inverse)
    inverse_out[0], inverse_out[1] = split(inverse[...])


def factor_scratch(size):
    return [pltpu.VMEM((size, size), F32), pltpu.VMEM((size, size), F32), pltpu.VMEM((B, B), F32), pltpu.VMEM((B, B), F32)]


def panel_call(kernel, order, blocks, third, with_link, extra):
    size = blocks.shape[-1]
    shapes = [jax.ShapeDtypeStruct((2, size, size), BF16)]
    if with_link:
        shapes.append(jax.ShapeDtypeStruct((size, size), BF16))
    return pl.pallas_call(
        kernel,
        out_shape=shapes,
        in_specs=[SMEM, VMEM, VMEM],
        out_specs=[VMEM] * len(shapes),
        scratch_shapes=factor_scratch(size) + extra,
        cost_estimate=pl.CostEstimate(flops=20_000_000_000, transcendentals=0, bytes_accessed=8_000_000),
    )(order, blocks, third)


def keep_of(pattern, lookup, panel, slot):
    return pattern[panel, lookup[slot]] == 1


def masked(value, pattern, lookup, panel, slot):
    blocks = [
        jnp.where(keep_of(pattern, lookup, panel, slot + i), value[i * B : (i + 1) * B], jnp.zeros((), value.dtype))
        for i in range(value.shape[0] // B)
    ]
    return jnp.concatenate(blocks, 0)


def solved(rows_first, rows_second, inverse_first, inverse_second, link):
    leading = (dot(rows_first, inverse_first[0], 1, 1) + dot(rows_first, inverse_first[1], 1, 1)).astype(BF16)
    high, low = split(rows_second.astype(F32) - dot(leading, link[...], 1, 1))
    later = dot(high, inverse_second[0], 1, 1) + dot(high, inverse_second[1], 1, 1) + dot(low, inverse_second[0], 1, 1)
    return leading, later.astype(BF16)


def started(sources, targets, semaphores):
    copies = [pltpu.make_async_copy(s, t, semaphores.at[i]) for i, (s, t) in enumerate(zip(sources, targets))]
    for copy in copies:
        copy.start()
    return copies


def own_kernel(
    order, place, pattern, lookup, own_hbm, inverse_first_hbm, link_hbm, inverse_second_hbm, row_rows_hbm, factor_out,
    own, inverse_first, link, inverse_second, row_rows, semaphores,
):
    first, second = order[0], order[1]
    height, size = row_rows.shape[1:]
    slot = place[0] * (height // B)
    pieces = own.shape[0]
    width = height // pieces
    copies = started(
        (own_hbm, inverse_first_hbm, link_hbm, inverse_second_hbm), (own, inverse_first, link, inverse_second), semaphores
    )
    for copy in copies:
        copy.wait()
    out = []
    step = CHUNK // width
    for start in range(0, height, CHUNK):
        part = pl.ds(start // width, step)
        rows_first, rows_second = [
            masked(own[part, panel].reshape(CHUNK, size), pattern, lookup, panel, slot + start // B)
            for panel in (first, second)
        ]
        here = slice(start, start + CHUNK)
        row_rows[0, here], row_rows[1, here] = solved(rows_first, rows_second, inverse_first, inverse_second, link)
        i = len(copies) + start // CHUNK
        copy = pltpu.make_async_copy(
            row_rows.at[:, pl.ds(start, CHUNK)], row_rows_hbm.at[:, pl.ds(start, CHUNK)], semaphores.at[i]
        )
        copy.start()
        out.append(copy)
    offset = pl.multiple_of(place[1] * width, 16)
    factor_out[first] = row_rows[0, pl.ds(offset, width), :]
    factor_out[second] = row_rows[1, pl.ds(offset, width), :]
    for copy in out:
        copy.wait()


def tail_kernel(
    order, place, pattern, lookup,
    mine_hbm, other_hbm, inverse_first_hbm, link_hbm, inverse_second_hbm, row_rows_hbm, trailing_hbm, updated_hbm,
    columns, inverse_first, link, inverse_second, row_rows, trailing, column_rows, updated, semaphores,
):
    first, second = order[0], order[1]
    core = place[2]
    height = trailing.shape[0]
    size = column_rows.shape[-1]
    slot = place[1] * (height // B)
    pieces = columns.shape[1]
    width = height // pieces
    copies = started(
        (mine_hbm, other_hbm, inverse_first_hbm, link_hbm, inverse_second_hbm, row_rows_hbm, trailing_hbm),
        (columns.at[core], columns.at[1 - core], inverse_first, link, inverse_second, row_rows, trailing),
        semaphores,
    )
    for copy in copies[:5]:
        copy.wait()
    step = CHUNK // width
    for start in range(0, height, CHUNK):
        part = pl.ds(start // width, step)
        rows_first, rows_second = [
            masked(columns[panel, part].reshape(CHUNK, size), pattern, lookup, panel, slot + start // B)
            for panel in (first, second)
        ]
        here = slice(start, start + CHUNK)
        column_rows[0, here], column_rows[1, here] = solved(
            rows_first, rows_second, inverse_first, inverse_second, link
        )
    for copy in copies[5:]:
        copy.wait()
    out = []
    for start in range(0, height, CHUNK):
        here = slice(start, start + CHUNK)
        result = trailing[here].astype(F32) - dot(row_rows[0, here], column_rows[0], 1, 1)
        result = result - dot(row_rows[1, here], column_rows[1], 1, 1)
        updated[here] = result.astype(BF16)
        chunk = pl.ds(start, CHUNK)
        copy = pltpu.make_async_copy(
            updated.at[chunk], updated_hbm.at[chunk], semaphores.at[len(copies) + start // CHUNK]
        )
        copy.start()
        out.append(copy)
    for copy in out:
        copy.wait()


def local(
    trailing,
    offdiagonal_panel_rows,
    pivot_diagonal_blocks,
    coupling,
    pattern,
    block_slot_lookup,
    elimination_sequence,
):
    depth, cores, columns = lax.axis_size("z"), lax.axis_size("core"), lax.axis_size("col")
    col_index, core = lax.axis_index("col"), lax.axis_index("core")
    place = jnp.stack([lax.axis_index("z") * cores + core, col_index, core]).astype(jnp.int32)
    rows = offdiagonal_panel_rows
    size = rows.shape[-1]
    height = trailing.shape[0]
    everywhere = ("z", "core", "col")

    def device(z, k, j):
        return (z * cores + k) * columns + j

    own = lax.all_to_all(jnp.broadcast_to(rows[None], (columns, *rows.shape)), "col", 0, 0)
    sent = []
    for panel in range(2):
        pairs = [
            (device(c // cores, c % cores, j), device(j, panel, c))
            for c in range(columns)
            for j in range(columns)
        ]
        sent.append(lax.ppermute(rows[panel], everywhere, pairs))
    piece = jnp.where(core == 0, sent[0], sent[1])
    mine = lax.all_to_all(jnp.broadcast_to(piece[None], (depth, *piece.shape)), "z", 0, 0)
    inverse_first, link = panel_call(
        first_kernel, elimination_sequence, pivot_diagonal_blocks, coupling, True,
        [pltpu.VMEM((size, size), BF16)],
    )
    (inverse_second,) = panel_call(second_kernel, elimination_sequence, pivot_diagonal_blocks, link, False, [])
    other = lax.ppermute(mine, "core", [(0, 1), (1, 0)])
    scalars = (elimination_sequence, place, pattern, block_slot_lookup)
    chunks = height // CHUNK
    square = pltpu.VMEM((2, size, size), BF16)
    solving = [square, pltpu.VMEM((size, size), BF16), square, pltpu.VMEM((2, height, size), BF16)]
    tile = pltpu.VMEM(trailing.shape, BF16)
    row_rows, factor_out = pl.pallas_call(
        own_kernel,
        out_shape=(jax.ShapeDtypeStruct((2, height, size), BF16), jax.ShapeDtypeStruct(rows.shape, BF16)),
        in_specs=[SMEM] * 4 + [ANY] * 4,
        out_specs=(ANY, VMEM),
        scratch_shapes=[pltpu.VMEM(own.shape, BF16)] + solving + [pltpu.SemaphoreType.DMA((4 + chunks,))],
        name="own_rows",
    )(*scalars, own, inverse_first, link, inverse_second)
    updated = pl.pallas_call(
        tail_kernel,
        out_shape=jax.ShapeDtypeStruct(trailing.shape, BF16),
        in_specs=[SMEM] * 4 + [ANY] * 7,
        out_specs=ANY,
        scratch_shapes=[pltpu.VMEM((2, *mine.shape), BF16)]
        + solving
        + [tile, pltpu.VMEM((2, height, size), BF16), tile, pltpu.SemaphoreType.DMA((7 + chunks,))],
        name="trailing_update",
    )(*scalars, mine, other, inverse_first, link, inverse_second, row_rows, trailing)
    return updated, factor_out


def solution(mesh):
    chips = mesh.shape["row"] // 2
    split_mesh = Mesh(mesh.devices.reshape(chips, 2, mesh.shape["col"]), ("z", "core", "col"))
    row = ("z", "core")
    panels = P(None, ("z", "core", "col"), None)
    return jax.shard_map(
        local,
        mesh=split_mesh,
        in_specs=(P(row, "col"), panels, P(), P(), P(), P(), P()),
        out_specs=(P(row, "col"), panels),
        check_vma=False,
    )
```

profile of v0, /device:TPU:1, one launch (start us, length us, event | category | flops | bytes accessed | tf_op | source)
XLA Modules:
  0.0 128.9 jit_solution(4441917021894720637)
XLA Ops:
  0.6 0.8 slice_bitcast_fusion
  1.5 4.5 %collective-permute-start = (bf16[48,512]{1,0:T(8,128)(2,1)S(1)}, bf16[48,512]{1,0:T(8,128)(2,1)S(1)}, u32[]{:S(2)}, u32[]{:S(2)}) collective-permute-start(bf16[48,512]{1,0:T(8,128)(2,1)S(1)} %get-tuple-element.11), channel_id=1, source_target_pairs={{0,0},{1,32},{2,64},{3,96},{4,128},{5,160},{6,192},{7,224},{8,256}... | collective-permute-start | bytes 147464 | tf_op jit(solution)/shard_map/ppermute | solution.py:305
  6.0 3.5 %collective-permute-start.1 = (bf16[48,512]{1,0:T(8,128)(2,1)S(1)}, bf16[48,512]{1,0:T(8,128)(2,1)S(1)}, u32[]{:S(2)}, u32[]{:S(2)}) collective-permute-start(bf16[48,512]{1,0:T(8,128)(2,1)S(1)} %get-tuple-element.10), channel_id=1, source_target_pairs={{0,16},{1,48},{2,80},{3,112},{4,144},{5,176},{6,208},{7,240},{8,27... | collective-permute-start | bytes 147464 | tf_op jit(solution)/shard_map/ppermute | solution.py:305
  9.5 0.0 collective-permute-done
  9.5 1.6 %collective-permute-done.1 = bf16[48,512]{1,0:T(8,128)(2,1)S(1)} collective-permute-done((bf16[48,512]{1,0:T(8,128)(2,1)S(1)}, bf16[48,512]{1,0:T(8,128)(2,1)S(1)}, u32[]{:S(2)}, u32[]{:S(2)}) %collective-permute-start.1) | collective-permute-done | bytes 49184 | tf_op jit(solution)/shard_map/ppermute | solution.py:305
  11.1 1.0 broadcast_in_dim.4
  12.1 29.1 %all-to-all-start = ((bf16[16,48,512]{2,1,0:T(8,128)(2,1)}), bf16[16,48,512]{2,1,0:T(8,128)(2,1)S(1)}, u32[]{:S(2)}, u32[]{:S(2)}) async-start(bf16[16,48,512]{2,1,0:T(8,128)(2,1)} %broadcast_in_dim.4), calls=%async_computation | async-start | bytes 1572864 | tf_op jit(solution)/shard_map/all_to_all | solution.py:307
  41.2 0.0 copy-start.3
  41.2 17.5 %shard_map.86 = (bf16[2,512,512]{2,1,0:T(8,128)(2,1)}, bf16[512,512]{1,0:T(8,128)(2,1)}) custom-call(s32[2]{0:T(128)} %order.7, bf16[2,512,512]{2,1,0:T(8,128)(2,1)} %blocks.3, bf16[512,512]{1,0:T(8,128)(2,1)} %coupling.1), custom_call_target="tpu_custom_call" | custom-call | flops 20000000000 | bytes 8000000 | tf_op jit(solution)/shard_map/pallas_call | solution.py:156
  58.7 16.8 %all-to-all-done.mine_hbm = bf16[16,48,512]{2,1,0:T(8,128)(2,1)S(1)} async-done(((bf16[16,48,512]{2,1,0:T(8,128)(2,1)}), bf16[16,48,512]{2,1,0:T(8,128)(2,1)S(1)}, u32[]{:S(2)}, u32[]{:S(2)}) %all-to-all-start) | async-done | bytes 786464 | tf_op jit(solution)/shard_map/all_to_all | solution.py:307
  75.5 0.0 copy-done.3
  75.5 0.0 copy-start.1
  75.5 1.4 %broadcast_in_dim.5 = bf16[16,2,48,512]{3,2,1,0:T(8,128)(2,1)} broadcast(bf16[2,48,512]{2,1,0:T(8,128)(2,1)S(1)} %copy-done.3), dimensions={1,2,3} | broadcast | bytes 1671168 | tf_op jit(solution)/shard_map/broadcast_in_dim | solution.py:297
  77.0 12.6 %all-to-all-start.1 = ((bf16[16,2,48,512]{3,2,1,0:T(8,128)(2,1)}), bf16[16,2,48,512]{3,2,1,0:T(8,128)(2,1)S(1)}, u32[]{:S(2)}, u32[]{:S(2)}) async-start(bf16[16,2,48,512]{3,2,1,0:T(8,128)(2,1)} %broadcast_in_dim.5), calls=%async_computation.1 | async-start | bytes 3145728 | tf_op jit(solution)/shard_map/all_to_all | solution.py:297
  89.6 0.0 copy-done.1
  89.6 4.1 %collective-permute-start.2 = (bf16[16,48,512]{2,1,0:T(8,128)(2,1)S(1)}, bf16[16,48,512]{2,1,0:T(8,128)(2,1)S(1)}, u32[]{:S(2)}, u32[]{:S(2)}) collective-permute-start(bf16[16,48,512]{2,1,0:T(8,128)(2,1)S(1)} %all-to-all-done.mine_hbm), channel_id=1, source_target_pairs={{0,16},{16,0},{1,17},{17,1},{2,18},{18,2},{3,19},{19,3},{4,20},{20... | collective-permute-start | bytes 2359304 | tf_op jit(solution)/shard_map/ppermute | solution.py:313
  93.7 16.9 %shard_map.87.inverse_second_hbm = bf16[2,512,512]{2,1,0:T(8,128)(2,1)} custom-call(s32[2]{0:T(128)} %order.7, bf16[2,512,512]{2,1,0:T(8,128)(2,1)} %blocks.3, bf16[512,512]{1,0:T(8,128)(2,1)} %get-tuple-element.7.link_ref.link_hbm), custom_call_target="tpu_custom_call" | custom-call | flops 20000000000 | bytes 8000000 | tf_op jit(solution)/shard_map/pallas_call | solution.py:156
  110.6 0.6 pad_add_fusion.place
  111.3 0.0 all-to-all-done.1.own_hbm
  111.3 0.0 copy-start
  111.3 1.1 copy-done
  112.4 7.3 %own_rows.1 = (bf16[2,768,512]{2,1,0:T(8,128)(2,1)}, bf16[2,48,512]{2,1,0:T(8,128)(2,1)}) custom-call(s32[2]{0:T(128)} %order.7, s32[3]{0:T(128)} %pad_add_fusion.place, s32[2,192]{1,0:T(2,128)} %pattern.3, s32[192]{0:T(256)} %lookup.3, bf16[16,2,48,512]{3,2,1,0:T(8,128)(2,1)} %copy-done, bf16[2,512,512]{2,1,0:T(8,128)(2,1)} %get-tuple-element.6.inverse_first_hbm, ...), custom_call_target="tpu_custom_call" | custom-call | tf_op jit(solution)/shard_map/own_rows/pallas_call | solution.py:319
  119.8 0.0 collective-permute-done.2.other_hbm
  119.8 0.0 copy-start.2
  119.8 0.9 copy-done.2
  120.6 8.1 %trailing_update.1 = bf16[768,768]{1,0:T(8,128)(2,1)} custom-call(s32[2]{0:T(128)} %order.7, s32[3]{0:T(128)} %pad_add_fusion.place, s32[2,192]{1,0:T(2,128)} %pattern.3, s32[192]{0:T(256)} %lookup.3, bf16[16,48,512]{2,1,0:T(8,128)(2,1)} %copy-done.1, bf16[16,48,512]{2,1,0:T(8,128)(2,1)} %copy-done.2, ...), custom_call_target="tpu_custom_call" | custom-call | tf_op jit(solution)/shard_map/trailing_update/pallas_call | solution.py:327
  (1 shorter events, 0.0 us)
Async XLA Ops:
  1.5 8.1 %collective-permute-start = (bf16[48,512]{1,0:T(8,128)(2,1)S(1)}, bf16[48,512]{1,0:T(8,128)(2,1)S(1)}, u32[]{:S(2)}, u32[]{:S(2)}) collective-permute-start(bf16[48,512]{1,0:T(8,128)(2,1)S(1)} %get-tuple-element.11), channel_id=1, source_target_pairs={{0,0},{1,32},{2,64},{3,96},{4,128},{5,160},{6,192},{7,224},{8,256}... | collective-permute-start | bytes 147464 | tf_op jit(solution)/shard_map/ppermute | solution.py:305
  6.0 5.2 %collective-permute-start.1 = (bf16[48,512]{1,0:T(8,128)(2,1)S(1)}, bf16[48,512]{1,0:T(8,128)(2,1)S(1)}, u32[]{:S(2)}, u32[]{:S(2)}) collective-permute-start(bf16[48,512]{1,0:T(8,128)(2,1)S(1)} %get-tuple-element.10), channel_id=1, source_target_pairs={{0,16},{1,48},{2,80},{3,112},{4,144},{5,176},{6,208},{7,240},{8,27... | collective-permute-start | bytes 147464 | tf_op jit(solution)/shard_map/ppermute | solution.py:305
  12.1 63.4 %all-to-all-start = ((bf16[16,48,512]{2,1,0:T(8,128)(2,1)}), bf16[16,48,512]{2,1,0:T(8,128)(2,1)S(1)}, u32[]{:S(2)}, u32[]{:S(2)}) async-start(bf16[16,48,512]{2,1,0:T(8,128)(2,1)} %broadcast_in_dim.4), calls=%async_computation | async-start | bytes 1572864 | tf_op jit(solution)/shard_map/all_to_all | solution.py:307
  41.2 34.3 %copy-start.3 = (bf16[2,48,512]{2,1,0:T(8,128)(2,1)S(1)}, bf16[2,48,512]{2,1,0:T(8,128)(2,1)}, u32[]{:S(2)}) copy-start(bf16[2,48,512]{2,1,0:T(8,128)(2,1)} %param.8) | copy-start | bytes 294916
  75.5 14.1 %copy-start.1 = (bf16[16,48,512]{2,1,0:T(8,128)(2,1)}, bf16[16,48,512]{2,1,0:T(8,128)(2,1)S(1)}, u32[]{:S(2)}) copy-start(bf16[16,48,512]{2,1,0:T(8,128)(2,1)S(1)} %all-to-all-done.mine_hbm) | copy-start | bytes 2359300
  77.0 34.3 %all-to-all-start.1 = ((bf16[16,2,48,512]{3,2,1,0:T(8,128)(2,1)}), bf16[16,2,48,512]{3,2,1,0:T(8,128)(2,1)S(1)}, u32[]{:S(2)}, u32[]{:S(2)}) async-start(bf16[16,2,48,512]{3,2,1,0:T(8,128)(2,1)} %broadcast_in_dim.5), calls=%async_computation.1 | async-start | bytes 3145728 | tf_op jit(solution)/shard_map/all_to_all | solution.py:297
  89.6 30.2 %collective-permute-start.2 = (bf16[16,48,512]{2,1,0:T(8,128)(2,1)S(1)}, bf16[16,48,512]{2,1,0:T(8,128)(2,1)S(1)}, u32[]{:S(2)}, u32[]{:S(2)}) collective-permute-start(bf16[16,48,512]{2,1,0:T(8,128)(2,1)S(1)} %all-to-all-done.mine_hbm), channel_id=1, source_target_pairs={{0,16},{16,0},{1,17},{17,1},{2,18},{18,2},{3,19},{19,3},{4,20},{20... | collective-permute-start | bytes 2359304 | tf_op jit(solution)/shard_map/ppermute | solution.py:313
  111.3 1.1 copy-start
  119.8 0.9 copy-start.2
where the time goes:
time: 129 us
  starting transfers between devices  53.9 us (42%)
  Pallas kernels  49.8 us (39%)
  waiting for transfers between devices  18.4 us (14%)
  local copies, waits for them, and re-layouts  5.25 us (4%)
    pallas_call x2, Pallas kernels, panel_call(): pl.pallas_call(kernel, out_shape=shapes, in_specs=[SMEM, VMEM, VMEM], out...  34.4 us
    all_to_all x1, starting transfers between devices, local(): lax.all_to_all(jnp.broadcast_to(piece[None], (depth, *piece.shape)), 'z',...  29.1 us
    all_to_all x1, waiting for transfers between devices, local(): lax.all_to_all(jnp.broadcast_to(piece[None], (depth, *piece.shape)), 'z',...  16.8 us
    all_to_all x1, starting transfers between devices, local(): lax.all_to_all(jnp.broadcast_to(rows[None], (columns, *rows.shape)), 'col...  12.6 us
    pallas_call x1, Pallas kernels, local(): pl.pallas_call(tail_kernel, out_shape=jax.ShapeDtypeStruct(trailing.shape...  8.05 us
    ppermute x2, starting transfers between devices, local(): sent.append(lax.ppermute(rows[panel], everywhere, pairs))  8.03 us
    pallas_call x1, Pallas kernels, local(): pl.pallas_call(own_kernel, out_shape=(jax.ShapeDtypeStruct((2, height, si...  7.34 us
    ppermute x1, starting transfers between devices, local(): other = lax.ppermute(mine, 'core', [(0, 1), (1, 0)])  4.08 us
  transfers between devices with their start and end apart: 5, of which 2 were waited for; matrix products, arithmetic and copies ran while one was open for 0% of the time, Pallas kernels for 32%

commit v1 on v0

--- a/solution.py
+++ b/solution.py
@@ -117,23 +117,37 @@
             inverse[rest, done] = inverse[rest, done] - dot_split(upper, inverse[here, done], 0, 0)
 
 
-def first_kernel(order, blocks, coupling, inverse_out, link_out, matrix, inverse, work, work_inverse, turned):
+def first_half_kernel(order, blocks, top_out, left_out, rest_out, matrix, inverse, work, work_inverse):
     first = order[0]
-    matrix[...] = blocks[first].astype(F32)
+    half = matrix.shape[0]
+    top, rest = slice(0, half), slice(half, 2 * half)
+    matrix[...] = blocks[first, top, top].astype(F32)
     factor(matrix, inverse, work, work_inverse)
-    high, low = split(inverse[...])
-    inverse_out[0], inverse_out[1] = high, low
-
-    @pl.when(first == 0)
+    upper = dot_split(inverse[...], blocks[first, top, rest].astype(F32), 1, 0)
+    top_out[...] = inverse[...]
+    left_out[...] = -dot_split(upper, inverse[...], 0, 0)
+    rest_out[...] = blocks[first, rest, rest].astype(F32) - dot_split(upper, upper, 0, 0)
+
+
+def first_kernel(order, coupling, top_ref, left_ref, rest_ref, inverse_out, link_out, matrix, inverse, work, work_inverse):
+    half = matrix.shape[0]
+    top, rest = slice(0, half), slice(half, 2 * half)
+    matrix[...] = rest_ref[...]
+    factor(matrix, inverse, work, work_inverse)
+    inverse_out[0, top, rest] = inverse_out[1, top, rest] = jnp.zeros((half, half), BF16)
+    inverse_out[0, top, top], inverse_out[1, top, top] = split(top_ref[...])
+    inverse_out[0, rest, rest], inverse_out[1, rest, rest] = split(inverse[...])
+    inverse_out[0, rest, top], inverse_out[1, rest, top] = split(dot_split(inverse[...], left_ref[...], 1, 0))
+
+    @pl.when(order[0] == 0)
     def _():
-        turned[...] = coupling[...]
-
-    @pl.when(first != 0)
+        kmat = coupling[...]
+        link_out[...] = (dot(kmat, inverse_out[0], 1, 1) + dot(kmat, inverse_out[1], 1, 1)).astype(BF16)
+
+    @pl.when(order[0] != 0)
     def _():
-        turned[...] = coupling[...].astype(F32).T.astype(BF16)
-
-    kmat = turned[...]
-    link_out[...] = (dot(kmat, high, 1, 1) + dot(kmat, low, 1, 1)).astype(BF16)
+        kmat = coupling[...].astype(F32).T.astype(BF16)
+        link_out[...] = (dot(kmat, inverse_out[0], 1, 1) + dot(kmat, inverse_out[1], 1, 1)).astype(BF16)
 
 
 def second_kernel(order, blocks, link_ref, inverse_out, matrix, inverse, work, work_inverse):
@@ -144,23 +158,15 @@
     inverse_out[0], inverse_out[1] = split(inverse[...])
 
 
-def factor_scratch(size):
-    return [pltpu.VMEM((size, size), F32), pltpu.VMEM((size, size), F32), pltpu.VMEM((B, B), F32), pltpu.VMEM((B, B), F32)]
-
-
-def panel_call(kernel, order, blocks, third, with_link, extra):
-    size = blocks.shape[-1]
-    shapes = [jax.ShapeDtypeStruct((2, size, size), BF16)]
-    if with_link:
-        shapes.append(jax.ShapeDtypeStruct((size, size), BF16))
+def panel_call(kernel, operands, shapes, size):
     return pl.pallas_call(
         kernel,
         out_shape=shapes,
-        in_specs=[SMEM, VMEM, VMEM],
+        in_specs=[SMEM] + [VMEM] * (len(operands) - 1),
         out_specs=[VMEM] * len(shapes),
-        scratch_shapes=factor_scratch(size) + extra,
-        cost_estimate=pl.CostEstimate(flops=20_000_000_000, transcendentals=0, bytes_accessed=8_000_000),
-    )(order, blocks, third)
+        scratch_shapes=[pltpu.VMEM((size, size), F32)] * 2 + [pltpu.VMEM((B, B), F32)] * 2,
+        cost_estimate=pl.CostEstimate(flops=10_000_000_000, transcendentals=0, bytes_accessed=4_000_000),
+    )(*operands)
 
 
 def keep_of(pattern, lookup, panel, slot):
@@ -305,11 +311,16 @@
         sent.append(lax.ppermute(rows[panel], everywhere, pairs))
     piece = jnp.where(core == 0, sent[0], sent[1])
     mine = lax.all_to_all(jnp.broadcast_to(piece[None], (depth, *piece.shape)), "z", 0, 0)
+    half = jax.ShapeDtypeStruct((size // 2, size // 2), F32)
+    inverse_shape = jax.ShapeDtypeStruct((2, size, size), BF16)
+    halves = panel_call(first_half_kernel, (elimination_sequence, pivot_diagonal_blocks), [half] * 3, size // 2)
     inverse_first, link = panel_call(
-        first_kernel, elimination_sequence, pivot_diagonal_blocks, coupling, True,
-        [pltpu.VMEM((size, size), BF16)],
-    )
-    (inverse_second,) = panel_call(second_kernel, elimination_sequence, pivot_diagonal_blocks, link, False, [])
+        first_kernel, (elimination_sequence, coupling, *halves),
+        [inverse_shape, jax.ShapeDtypeStruct((size, size), BF16)], size // 2,
+    )
+    (inverse_second,) = panel_call(
+        second_kernel, (elimination_sequence, pivot_diagonal_blocks, link), [inverse_shape], size
+    )
     other = lax.ppermute(mine, "core", [(0, 1), (1, 0)])
     scalars = (elimination_sequence, place, pattern, block_slot_lookup)
     chunks = height // CHUNK

time: 129 us -> 139 us (1.078)
  waiting for transfers between devices: 18.4 us -> 25.8 us
  Pallas kernels: 49.8 us -> 52.1 us
    all_to_all x1, waiting for transfers between devices: 16.8 us -> 24.2 us  [local(): lax.all_to_all(jnp.broadcast_to(piece[None], (depth, *piece.shape)), 'z',...]
    pallas_call x2 -> x3, Pallas kernels: 34.4 us -> 36.7 us  [panel_call(): pl.pallas_call(kernel, out_shape=shapes, in_specs=[SMEM] + [VMEM] * (len(...]
where the time goes in v1:
time: 139 us; the launch traced here: 138 us
  starting transfers between devices  53.9 us (39%)
  Pallas kernels  52.1 us (37%)
  waiting for transfers between devices  25.8 us (19%)
  local copies, waits for them, and re-layouts  5.22 us (4%)
    pallas_call x3, Pallas kernels, panel_call(): pl.pallas_call(kernel, out_shape=shapes, in_specs=[SMEM] + [VMEM] * (len(...  36.7 us
    all_to_all x1, starting transfers between devices, local(): lax.all_to_all(jnp.broadcast_to(piece[None], (depth, *piece.shape)), 'z',...  29.1 us
    all_to_all x1, waiting for transfers between devices, local(): lax.all_to_all(jnp.broadcast_to(piece[None], (depth, *piece.shape)), 'z',...  24.2 us
    all_to_all x1, starting transfers between devices, local(): lax.all_to_all(jnp.broadcast_to(rows[None], (columns, *rows.shape)), 'col...  12.6 us
    pallas_call x1, Pallas kernels, local(): pl.pallas_call(tail_kernel, out_shape=jax.ShapeDtypeStruct(trailing.shape...  8.04 us
    ppermute x2, starting transfers between devices, local(): sent.append(lax.ppermute(rows[panel], everywhere, pairs))  8.03 us
    pallas_call x1, Pallas kernels, local(): pl.pallas_call(own_kernel, out_shape=(jax.ShapeDtypeStruct((2, height, si...  7.34 us
    ppermute x1, starting transfers between devices, local(): other = lax.ppermute(mine, 'core', [(0, 1), (1, 0)])  4.06 us
  transfers between devices with their start and end apart: 5, of which 2 were waited for; matrix products, arithmetic and copies ran while one was open for 0% of the time, Pallas kernels for 32%

profile of v1, /device:TPU:1, one launch (start us, length us, event | category | flops | bytes accessed | tf_op | source)
XLA Modules:
  0.0 138.4 jit_solution(5392535828743204327)
XLA Ops:
  0.6 0.8 slice_bitcast_fusion
  1.5 4.5 %collective-permute-start = (bf16[48,512]{1,0:T(8,128)(2,1)S(1)}, bf16[48,512]{1,0:T(8,128)(2,1)S(1)}, u32[]{:S(2)}, u32[]{:S(2)}) collective-permute-start(bf16[48,512]{1,0:T(8,128)(2,1)S(1)} %get-tuple-element.17), channel_id=1, source_target_pairs={{0,0},{1,32},{2,64},{3,96},{4,128},{5,160},{6,192},{7,224},{8,256}... | collective-permute-start | bytes 147464 | tf_op jit(solution)/shard_map/ppermute | solution.py:311
  6.0 3.5 %collective-permute-start.1 = (bf16[48,512]{1,0:T(8,128)(2,1)S(1)}, bf16[48,512]{1,0:T(8,128)(2,1)S(1)}, u32[]{:S(2)}, u32[]{:S(2)}) collective-permute-start(bf16[48,512]{1,0:T(8,128)(2,1)S(1)} %get-tuple-element.16), channel_id=1, source_target_pairs={{0,16},{1,48},{2,80},{3,112},{4,144},{5,176},{6,208},{7,240},{8,27... | collective-permute-start | bytes 147464 | tf_op jit(solution)/shard_map/ppermute | solution.py:311
  9.5 0.0 collective-permute-done
  9.5 1.6 %collective-permute-done.1 = bf16[48,512]{1,0:T(8,128)(2,1)S(1)} collective-permute-done((bf16[48,512]{1,0:T(8,128)(2,1)S(1)}, bf16[48,512]{1,0:T(8,128)(2,1)S(1)}, u32[]{:S(2)}, u32[]{:S(2)}) %collective-permute-start.1) | collective-permute-done | bytes 49184 | tf_op jit(solution)/shard_map/ppermute | solution.py:311
  11.1 1.0 broadcast_in_dim.4
  12.1 29.1 %all-to-all-start = ((bf16[16,48,512]{2,1,0:T(8,128)(2,1)}), bf16[16,48,512]{2,1,0:T(8,128)(2,1)S(1)}, u32[]{:S(2)}, u32[]{:S(2)}) async-start(bf16[16,48,512]{2,1,0:T(8,128)(2,1)} %broadcast_in_dim.4), calls=%async_computation | async-start | bytes 1572864 | tf_op jit(solution)/shard_map/all_to_all | solution.py:313
  41.2 0.6 pad_add_fusion.place
  41.8 0.0 copy-start.3
  41.8 9.5 %shard_map.86 = (f32[256,256]{1,0:T(8,128)}, f32[256,256]{1,0:T(8,128)}, f32[256,256]{1,0:T(8,128)}) custom-call(s32[2]{0:T(128)} %order.9, bf16[2,512,512]{2,1,0:T(8,128)(2,1)} %blocks.3), custom_call_target="tpu_custom_call" | custom-call | flops 10000000000 | bytes 4000000 | tf_op jit(solution)/shard_map/pallas_call | solution.py:162
  51.3 24.2 %all-to-all-done.mine_hbm = bf16[16,48,512]{2,1,0:T(8,128)(2,1)S(1)} async-done(((bf16[16,48,512]{2,1,0:T(8,128)(2,1)}), bf16[16,48,512]{2,1,0:T(8,128)(2,1)S(1)}, u32[]{:S(2)}, u32[]{:S(2)}) %all-to-all-start) | async-done | bytes 786464 | tf_op jit(solution)/shard_map/all_to_all | solution.py:313
  75.5 0.0 copy-done.3
  75.5 0.0 copy-start.1
  75.5 1.4 %broadcast_in_dim.5 = bf16[16,2,48,512]{3,2,1,0:T(8,128)(2,1)} broadcast(bf16[2,48,512]{2,1,0:T(8,128)(2,1)S(1)} %copy-done.3), dimensions={1,2,3} | broadcast | bytes 1671168 | tf_op jit(solution)/shard_map/broadcast_in_dim | solution.py:303
  76.9 12.6 %all-to-all-start.1 = ((bf16[16,2,48,512]{3,2,1,0:T(8,128)(2,1)}), bf16[16,2,48,512]{3,2,1,0:T(8,128)(2,1)S(1)}, u32[]{:S(2)}, u32[]{:S(2)}) async-start(bf16[16,2,48,512]{3,2,1,0:T(8,128)(2,1)} %broadcast_in_dim.5), calls=%async_computation.1 | async-start | bytes 3145728 | tf_op jit(solution)/shard_map/all_to_all | solution.py:303
  89.6 10.2 %shard_map.87 = (bf16[2,512,512]{2,1,0:T(8,128)(2,1)}, bf16[512,512]{1,0:T(8,128)(2,1)}) custom-call(s32[2]{0:T(128)} %order.9, bf16[512,512]{1,0:T(8,128)(2,1)} %coupling.1, f32[256,256]{1,0:T(8,128)} %get-tuple-element.9.top_ref, f32[256,256]{1,0:T(8,128)} %get-tuple-element.10.left_ref, f32[256,256]{1,0:T(8,128)} %get-tuple-element.11.rest_ref), custom_call_target="tpu_custom_call" | custom-call | flops 10000000000 | bytes 4000000 | tf_op jit(solution)/shard_map/pallas_call | solution.py:162
  99.8 0.0 copy-done.1
  99.8 4.1 %collective-permute-start.2 = (bf16[16,48,512]{2,1,0:T(8,128)(2,1)S(1)}, bf16[16,48,512]{2,1,0:T(8,128)(2,1)S(1)}, u32[]{:S(2)}, u32[]{:S(2)}) collective-permute-start(bf16[16,48,512]{2,1,0:T(8,128)(2,1)S(1)} %all-to-all-done.mine_hbm), channel_id=1, source_target_pairs={{0,16},{16,0},{1,17},{17,1},{2,18},{18,2},{3,19},{19,3},{4,20},{20... | collective-permute-start | bytes 2359304 | tf_op jit(solution)/shard_map/ppermute | solution.py:324
  103.9 17.0 %shard_map.88.inverse_second_hbm = bf16[2,512,512]{2,1,0:T(8,128)(2,1)} custom-call(s32[2]{0:T(128)} %order.9, bf16[2,512,512]{2,1,0:T(8,128)(2,1)} %blocks.3, bf16[512,512]{1,0:T(8,128)(2,1)} %get-tuple-element.13.link_ref.link_hbm), custom_call_target="tpu_custom_call" | custom-call | flops 10000000000 | bytes 4000000 | tf_op jit(solution)/shard_map/pallas_call | solution.py:162
  120.8 0.0 all-to-all-done.1.own_hbm
  120.8 0.0 copy-start
  120.8 1.1 copy-done
  122.0 7.3 %own_rows.1 = (bf16[2,768,512]{2,1,0:T(8,128)(2,1)}, bf16[2,48,512]{2,1,0:T(8,128)(2,1)}) custom-call(s32[2]{0:T(128)} %order.9, s32[3]{0:T(128)} %pad_add_fusion.place, s32[2,192]{1,0:T(2,128)} %pattern.3, s32[192]{0:T(256)} %lookup.3, bf16[16,2,48,512]{3,2,1,0:T(8,128)(2,1)} %copy-done, bf16[2,512,512]{2,1,0:T(8,128)(2,1)} %get-tuple-element.12.inverse_first_hbm, ...), custom_call_target="tpu_custom_call" | custom-call | tf_op jit(solution)/shard_map/own_rows/pallas_call | solution.py:330
  129.3 0.0 collective-permute-done.2.other_hbm
  129.3 0.0 copy-start.2
  129.3 0.9 copy-done.2
  130.2 8.0 %trailing_update.1 = bf16[768,768]{1,0:T(8,128)(2,1)} custom-call(s32[2]{0:T(128)} %order.9, s32[3]{0:T(128)} %pad_add_fusion.place, s32[2,192]{1,0:T(2,128)} %pattern.3, s32[192]{0:T(256)} %lookup.3, bf16[16,48,512]{2,1,0:T(8,128)(2,1)} %copy-done.1, bf16[16,48,512]{2,1,0:T(8,128)(2,1)} %copy-done.2, ...), custom_call_target="tpu_custom_call" | custom-call | tf_op jit(solution)/shard_map/trailing_update/pallas_call | solution.py:338
  (1 shorter events, 0.0 us)
Async XLA Ops:
  1.5 8.1 %collective-permute-start = (bf16[48,512]{1,0:T(8,128)(2,1)S(1)}, bf16[48,512]{1,0:T(8,128)(2,1)S(1)}, u32[]{:S(2)}, u32[]{:S(2)}) collective-permute-start(bf16[48,512]{1,0:T(8,128)(2,1)S(1)} %get-tuple-element.17), channel_id=1, source_target_pairs={{0,0},{1,32},{2,64},{3,96},{4,128},{5,160},{6,192},{7,224},{8,256}... | collective-permute-start | bytes 147464 | tf_op jit(solution)/shard_map/ppermute | solution.py:311
  6.0 5.2 %collective-permute-start.1 = (bf16[48,512]{1,0:T(8,128)(2,1)S(1)}, bf16[48,512]{1,0:T(8,128)(2,1)S(1)}, u32[]{:S(2)}, u32[]{:S(2)}) collective-permute-start(bf16[48,512]{1,0:T(8,128)(2,1)S(1)} %get-tuple-element.16), channel_id=1, source_target_pairs={{0,16},{1,48},{2,80},{3,112},{4,144},{5,176},{6,208},{7,240},{8,27... | collective-permute-start | bytes 147464 | tf_op jit(solution)/shard_map/ppermute | solution.py:311
  12.1 63.4 %all-to-all-start = ((bf16[16,48,512]{2,1,0:T(8,128)(2,1)}), bf16[16,48,512]{2,1,0:T(8,128)(2,1)S(1)}, u32[]{:S(2)}, u32[]{:S(2)}) async-start(bf16[16,48,512]{2,1,0:T(8,128)(2,1)} %broadcast_in_dim.4), calls=%async_computation | async-start | bytes 1572864 | tf_op jit(solution)/shard_map/all_to_all | solution.py:313
  41.8 33.7 %copy-start.3 = (bf16[2,48,512]{2,1,0:T(8,128)(2,1)S(1)}, bf16[2,48,512]{2,1,0:T(8,128)(2,1)}, u32[]{:S(2)}) copy-start(bf16[2,48,512]{2,1,0:T(8,128)(2,1)} %param.8) | copy-start | bytes 294916
  75.5 24.3 %copy-start.1 = (bf16[16,48,512]{2,1,0:T(8,128)(2,1)}, bf16[16,48,512]{2,1,0:T(8,128)(2,1)S(1)}, u32[]{:S(2)}) copy-start(bf16[16,48,512]{2,1,0:T(8,128)(2,1)S(1)} %all-to-all-done.mine_hbm) | copy-start | bytes 2359300
  76.9 43.9 %all-to-all-start.1 = ((bf16[16,2,48,512]{3,2,1,0:T(8,128)(2,1)}), bf16[16,2,48,512]{3,2,1,0:T(8,128)(2,1)S(1)}, u32[]{:S(2)}, u32[]{:S(2)}) async-start(bf16[16,2,48,512]{3,2,1,0:T(8,128)(2,1)} %broadcast_in_dim.5), calls=%async_computation.1 | async-start | bytes 3145728 | tf_op jit(solution)/shard_map/all_to_all | solution.py:303
  99.8 29.5 %collective-permute-start.2 = (bf16[16,48,512]{2,1,0:T(8,128)(2,1)S(1)}, bf16[16,48,512]{2,1,0:T(8,128)(2,1)S(1)}, u32[]{:S(2)}, u32[]{:S(2)}) collective-permute-start(bf16[16,48,512]{2,1,0:T(8,128)(2,1)S(1)} %all-to-all-done.mine_hbm), channel_id=1, source_target_pairs={{0,16},{16,0},{1,17},{17,1},{2,18},{18,2},{3,19},{19,3},{4,20},{20... | collective-permute-start | bytes 2359304 | tf_op jit(solution)/shard_map/ppermute | solution.py:324
  120.8 1.1 copy-start
  129.3 0.9 copy-start.2
